TPU v7x, 32 devices: a whole 2x2x4 slice. The times are simulated.
32 devices in a mesh: grp: 2 (over y), frm: 4 (over z), row: 4 (over x, core).
Axes of the slice: x: 2, y: 2, z: 4, core: 2. Of those that a mesh axis runs over, the one named last changes fastest.
Arguments:
- queries: bfloat16 [16, 8, 128, 2240], P(('grp', 'frm'), 'row'), parts along dimension 0, may hold values from -6 to 6
- keys: bfloat16 [16, 8, 128, 2240], P(('grp', 'frm'), 'row'), parts along dimension 0, may hold values from -6 to 6
- values: bfloat16 [16, 8, 128, 2240], P(('grp', 'frm'), 'row'), parts along dimension 0, may hold values from -6 to 6
- flags: int32 [16], P(('grp', 'frm')), parts along dimension 0, may hold values 0 or 1
- blocks: int32 [16], P(('grp', 'frm')), parts along dimension 0, may hold values from 0 to 2, as said below
- out_weight: bfloat16 [2240, 2240], P('frm'), may hold values from -0.125 to 0.125
- norm_gain: float32 [2240], replicated, may hold values from 0.1 to 1.9
Outputs:
- projected: bfloat16 [16, 8, 128, 2240], P(('grp', 'frm'), 'row'), parts along dimension 0
There are 2 independent parts, one for each index of `grp`. A program takes and returns all parts, laid end to end along the dimension named above; an argument that names none is the same for every part. Nothing has to cross between parts.
Inputs may be any that keep to these rules, and one draw needn't show every extreme that they name: `flags`: 1 marks a clean frame, 0 a noisy one. `blocks`: within the 8 frames of one group, block numbers never fall and each block is 1 to 4 consecutive frames, some block exactly 4; every number from 0 to 2 occurs.
All inputs are finite; a program needn't handle non-finite values. No bound on the sum of `flags` on one device may be relied on, other than what follows from the above.
Results may differ from a plain program's by a relative error of at most 0.0049.
Values may be sent and summed in bfloat16 or wider, within the bound.
No kernel may reach another device: no remote copies, remote signals or barrier semaphores. Data moves between devices by JAX's collectives and lax.ppermute only.
A program may use at most 192 MiB of HBM per device.

v0:
```python
import jax
import jax.numpy as jnp
from jax import lax
from jax.sharding import PartitionSpec as P

HEADS = 20
HD = 112
norm_eps = 1e-06


def entering(part, axis, combine, identity):
    place = lax.axis_index(axis)
    gathered = jax.tree.map(lambda a: lax.all_gather(a, axis), part)
    state = jax.tree.map(lambda a, e: jnp.zeros_like(a) + jnp.asarray(e, a.dtype), part, identity)

    def one(step, state):
        return combine(
            state, jax.tree.map(lambda a: lax.dynamic_index_in_dim(a, step, 0, False), gathered)
        )

    return lax.fori_loop(0, place, one, state)


def combine(earlier, later):
    closed_a, opened_a, latest_a = earlier
    closed_b, opened_b, latest_b = later
    advance = (latest_a < latest_b).astype(jnp.float32)
    return (
        closed_a + closed_b + advance * opened_a,
        opened_b + (1.0 - advance) * opened_a,
        jnp.maximum(latest_a, latest_b),
    )


def empty_carry(length):
    return (
        jnp.zeros((length,), jnp.float32),
        jnp.zeros((length,), jnp.float32),
        jnp.full((1,), -1.0, jnp.float32),
    )


def frame_element(frame_states, flag_values, block_values, frame_idx):
    length = frame_states.shape[1]
    return (
        jnp.zeros((length,), jnp.float32),
        flag_values[frame_idx] * frame_states[frame_idx],
        block_values[frame_idx : frame_idx + 1],
    )


def fold_frames(frame_states, flag_values, block_values):
    running = empty_carry(frame_states.shape[1])
    for frame_idx in range(frame_states.shape[0]):
        running = combine(
            running, frame_element(frame_states, flag_values, block_values, frame_idx)
        )
    return running


def read_frames(prefix, frame_states, flag_values, block_values):
    running = prefix
    collected = []
    for frame_idx in range(frame_states.shape[0]):
        advance = (running[2] < block_values[frame_idx : frame_idx + 1]).astype(jnp.float32)
        select = jnp.maximum(advance, flag_values[frame_idx])
        collected.append(running[0] + select * running[1] + frame_states[frame_idx])
        running = combine(
            running, frame_element(frame_states, flag_values, block_values, frame_idx)
        )
    return jnp.stack(collected)


def local(queries, keys, values, flags, blocks, out_weight, norm_gain):
    frames, lat_rows, lat_cols, model_width = queries.shape
    tokens = lat_rows * lat_cols
    key_pos = jax.nn.relu(keys).reshape(frames, tokens, HEADS, HD)
    value_heads = values.reshape(frames, tokens, HEADS, HD)
    partial_value = jnp.einsum(
        "ftha,fthb->fhab", key_pos, value_heads, preferred_element_type=jnp.float32
    )
    partial_value = partial_value.reshape(frames, HEADS * HD * HD)
    flag_values = flags.astype(jnp.float32)
    block_values = blocks.astype(jnp.float32)
    summed = lax.psum(partial_value, "row")
    totals = fold_frames(summed, flag_values, block_values)
    prefix = entering(
        (totals[0], totals[1], totals[2]), "frm", combine, empty_carry(summed.shape[1])
    )
    read_states = read_frames(prefix, summed, flag_values, block_values)
    read_tensor = read_states.reshape(frames, HEADS, HD, HD)
    query_pos = jax.nn.relu(queries).reshape(frames, tokens, HEADS, HD).astype(jnp.float32)
    attended = jnp.einsum(
        "ftha,fhab->fthb", query_pos, read_tensor, precision=lax.Precision.HIGHEST
    )
    inv_rms = lax.rsqrt(jnp.mean(attended * attended, axis=-1, keepdims=True) + norm_eps)
    gain_table = norm_gain.reshape(HEADS, HD)
    normed = (
        (attended * inv_rms * gain_table).astype(jnp.bfloat16).reshape(frames * tokens, model_width)
    )
    projected = jnp.dot(
        normed,
        lax.all_gather(out_weight, "frm", axis=0, tiled=True),
        preferred_element_type=jnp.float32,
    )
    return projected.astype(jnp.bfloat16).reshape(frames, lat_rows, lat_cols, model_width)


def solution(mesh):
    in_specs = (
        P(("grp", "frm"), "row", None, None),
        P(("grp", "frm"), "row", None, None),
        P(("grp", "frm"), "row", None, None),
        P(("grp", "frm")),
        P(("grp", "frm")),
        P("frm", None),
        P(),
    )
    out_specs = P(("grp", "frm"), "row", None, None)
    return jax.shard_map(local, mesh=mesh, in_specs=in_specs, out_specs=out_specs, check_vma=False)
```

profile of v0, /device:TPU:0, one launch (start us, length us, event | category | flops | bytes accessed | tf_op | source)
XLA Modules:
  0.0 476.6 jit_solution(3732474962754750551)
XLA Ops:
  6.5 1.8 broadcast_maximum_fusion.1
  8.3 10.3 %copy.16 = bf16[2,2,128,2240]{2,1,3,0:T(2,128)(2,1)} copy(bf16[2,2,128,2240]{2,3,1,0:T(8,128)(2,1)S(1)} %broadcast_maximum_fusion.1) | data formatting | bytes 4587520 | tf_op jit(solution)/shard_map/jit(relu)/max | solution.py:77
  18.7 5.2 %reshape.37 = bf16[2,256,20,112]{1,3,2,0:T(8,128)(2,1)S(1)} reshape(bf16[2,2,128,2240]{2,1,3,0:T(2,128)(2,1)} %copy.16) | data formatting | bytes 4587520 | tf_op jit(solution)/shard_map/reshape | solution.py:77
  23.9 12.6 %copy.17 = bf16[2,2,128,2240]{2,1,3,0:T(2,128)(2,1)} copy(bf16[2,2,128,2240]{2,3,1,0:T(8,128)(2,1)} %param.11) | data formatting | bytes 4587520 | tf_op args[2]
  36.5 6.2 %reshape.38 = bf16[2,256,20,112]{1,3,2,0:T(8,128)(2,1)} reshape(bf16[2,2,128,2240]{2,1,3,0:T(2,128)(2,1)} %copy.17) | data formatting | bytes 4587520 | tf_op jit(solution)/shard_map/reshape | solution.py:78
  42.7 3.8 fusion.10
  46.5 5.6 %reshape.39 = f32[2,250880]{1,0:T(2,128)} reshape(f32[2,20,112,112]{3,2,1,0:T(8,128)} %fusion.10) | data formatting | bytes 4014080 | tf_op jit(solution)/shard_map/reshape | solution.py:82
  52.1 0.6 dynamic-slice
  52.7 1.3 maximum_dynamic-update-slice_fusion
  55.9 0.6 fusion.9
  56.6 48.6 %all-reduce.3.cloned.1.call-done = f32[2,250880]{1,0:T(2,128)} async-done(((f32[2,250880]{1,0:T(2,128)}), f32[2,250880]{1,0:T(2,128)}) %all-reduce.3.cloned.1.call-update) | async-done | bytes 2007056 | tf_op jit(solution)/shard_map/psum | solution.py:85
  105.1 8.0 %fusion.8 = (f32[1,250880]{1,0:T(1,128)S(1)}, f32[1,1,250880]{2,1,0:T(1,128)}, f32[1,1,250880]{2,1,0:T(1,128)}, f32[1,250880]{1,0:T(1,128)}) fusion(f32[2,250880]{1,0:T(2,128)} %all-reduce.3.cloned.1.call-done, f32[]{:T(128)} %bitcast.7, f32[]{:T(128)} %bitcast.6, f32[]{:T(128)} %bitcast.5, f32[]{:T(128)} %bitcast.12, f32[]{:T(128)} %bitcast.11), kind=kLoop, calls=%fused_computation.27 | loop fusion | flops 1505280 | bytes 6021140 | tf_op jit(solution)/shard_map/slice | solution.py:47
  113.1 0.7 all-gather.9.cloned.1.call-update
  113.9 0.5 all-gather.7.cloned.1.call-update
  114.4 11.9 %all-reduce = f32[4]{0:T(128)S(1)} all-reduce(f32[4]{0:T(128)S(1)} %get-tuple-element.81), channel_id=2, replica_groups=mesh['grp'=2,'frm'=4,'row'=4] {'frm'}, use_global_device_ids=true, to_apply=%add | all-reduce | flops 4 | bytes 32
  126.4 10.1 %copy.20 = bf16[2,2,128,2240]{2,1,3,0:T(2,128)(2,1)S(1)} copy(bf16[2,2,128,2240]{2,3,1,0:T(8,128)(2,1)S(1)} %broadcast_maximum_fusion) | data formatting | bytes 4587520 | tf_op jit(solution)/shard_map/jit(relu)/max | solution.py:92
  136.5 2.7 reshape.40
  139.3 51.7 %all-gather.11.cloned.1.call-done = f32[4,1,250880]{2,1,0:T(1,128)} async-done(((f32[1,1,250880]{2,1,0:T(1,128)}), f32[4,1,250880]{2,1,0:T(1,128)}) %all-gather.11.cloned.1.call-update) | async-done | bytes 4014096 | tf_op jit(solution)/shard_map/all_gather | solution.py:13
  191.1 5.5 %copy.28 = f32[4,1,250880]{2,0,1:T(4,128)} copy(f32[4,1,250880]{2,1,0:T(1,128)} %all-gather.11.cloned.1.call-done) | data formatting | bytes 8028160
  196.5 72.4 %all-gather.9.cloned.1.call-done = f32[4,1,250880]{2,1,0:T(1,128)} async-done(((f32[1,1,250880]{2,1,0:T(1,128)}), f32[4,1,250880]{2,1,0:T(1,128)}) %all-gather.9.cloned.1.call-update) | async-done | bytes 4014096 | tf_op jit(solution)/shard_map/all_gather | solution.py:13
  268.9 5.5 %copy.29 = f32[4,1,250880]{2,0,1:T(4,128)} copy(f32[4,1,250880]{2,1,0:T(1,128)} %all-gather.9.cloned.1.call-done) | data formatting | bytes 8028160
  277.9 3.6 add_add_fusion.1
  281.5 1.9 stack.9
  283.8 3.0 stack.10
  286.7 2.7 copy.19
  289.4 3.7 fusion
  293.2 0.7 fusion.2
  293.9 2.4 copy.21
  296.7 153.4 %all-gather.7.cloned.1.call-done = bf16[2240,2240]{1,0:T(8,128)(2,1)} async-done(((bf16[560,2240]{1,0:T(8,128)(2,1)}), bf16[2240,2240]{1,0:T(8,128)(2,1)}) %all-gather.7.cloned.1.call-update) | async-done | bytes 10035216 | tf_op jit(solution)/shard_map/all_gather | solution.py:103
  450.1 13.4 %convolution_convert_fusion = bf16[512,2240]{0,1:T(8,128)(2,1)} fusion(bf16[512,2240]{0,1:T(8,128)(2,1)S(1)} %bitcast.74, bf16[2240,2240]{1,0:T(8,128)(2,1)} %all-gather.7.cloned.1.call-done), kind=kOutput, calls=%fused_computation.10 | convolution fusion | flops 5139169280 | bytes 14622720 | tf_op jit(solution)/shard_map/dot_general | solution.py:101
  463.6 4.8 %reshape.42 = bf16[2,2,128,2240]{2,1,0,3:T(2,128)(2,1)S(1)} reshape(bf16[512,2240]{0,1:T(8,128)(2,1)} %convolution_convert_fusion) | data formatting | bytes 4587520 | tf_op jit(solution)/shard_map/reshape | solution.py:106
  468.4 1.7 copy.22
  (29 shorter events, 1.6 us)
Async XLA Ops:
  6.5 98.6 %all-reduce.3.cloned.1.call-start = ((), (), s32[]{:S(2)}) async-start(), calls=%async_computation | async-start | bytes 4014080 | tf_op jit(solution)/shard_map/psum | solution.py:85
  46.5 5.6 %copy-start.3 = (s32[2]{0:T(128)S(1)}, s32[2]{0:T(128)}, u32[]{:S(2)}) copy-start(s32[2]{0:T(128)} %param.13) | copy-start | bytes 28
  46.5 5.7 %copy-start.5 = (u32[32]{0:T(128)S(1)}, u32[32]{0:T(128)}, u32[]{:S(2)}) copy-start(u32[32]{0:T(128)} %constant.52) | copy-start | bytes 388
  46.5 9.4 %copy-start.4 = (s32[2]{0:T(128)S(1)}, s32[2]{0:T(128)}, u32[]{:S(2)}) copy-start(s32[2]{0:T(128)} %param.12) | copy-start | bytes 28
  52.0 139.0 %all-gather.11.cloned.1.call-start = ((), (), s32[]{:S(2)}) async-start(), calls=%async_computation.3 | async-start | bytes 5017600 | tf_op jit(solution)/shard_map/all_gather | solution.py:13
  113.1 13.2 %copy-start.1 = (bf16[2,2,128,2240]{2,3,1,0:T(8,128)(2,1)S(1)}, bf16[2,2,128,2240]{2,3,1,0:T(8,128)(2,1)}, u32[]{:S(2)}) copy-start(bf16[2,2,128,2240]{2,3,1,0:T(8,128)(2,1)} %param.9) | copy-start | bytes 6881284
  113.1 155.8 %all-gather.9.cloned.1.call-start = ((), (), s32[]{:S(2)}) async-start(), calls=%async_computation.2 | async-start | bytes 5017600 | tf_op jit(solution)/shard_map/all_gather | solution.py:13
  113.8 336.3 %all-gather.7.cloned.1.call-start = ((), (), s32[]{:S(2)}) async-start(), calls=%async_computation.1 | async-start | bytes 12902400 | tf_op jit(solution)/shard_map/all_gather | solution.py:103
  136.5 2.8 copy-start.2
  283.8 5.7 %copy-start = (bf16[2,256,20,112]{1,3,2,0:T(8,128)(2,1)S(1)}, bf16[2,256,20,112]{1,3,2,0:T(8,128)(2,1)}, u32[]{:S(2)}) copy-start(bf16[2,256,20,112]{1,3,2,0:T(8,128)(2,1)} %reshape.40) | copy-start | bytes 6881284
Sparse Core Ops, SparseCore 0:
  52.2 52.9 all-reduce.2
  113.2 77.8 all-gather.10
  192.6 76.2 all-gather.8
  270.3 179.7 all-gather.6
where the time goes:
time: 477 us
  waiting for transfers between devices  327 us (69%)
  local copies, waits for them, and re-layouts  82.4 us (17%)
  matrix products  21 us (4%)
  between operations  18.3 us (4%)
  other arithmetic  15.5 us (3%)
  blocking collectives  11.9 us (2%)
    all_gather x1, waiting for transfers between devices, local(): lax.all_gather(out_weight, 'frm', axis=0, tiled=True)  153 us
    all_gather x2, waiting for transfers between devices, entering(): gathered = jax.tree.map(lambda a: lax.all_gather(a, axis), part)  124 us
    psum x1, waiting for transfers between devices, local(): summed = lax.psum(partial_value, 'row')  48.6 us
    unnamed x18, local copies, waits for them, and re-layouts  24.6 us
    dot_general x1, matrix products, local(): jnp.dot(normed, lax.all_gather(out_weight, 'frm', axis=0, tiled=True), pr...  13.4 us
    unnamed x1, blocking collectives  11.9 us
    max x1, local copies, waits for them, and re-layouts, local(): key_pos = jax.nn.relu(keys).reshape(frames, tokens, HEADS, HD)  10.3 us
    max x1, local copies, waits for them, and re-layouts, local(): jax.nn.relu(queries).reshape(frames, tokens, HEADS, HD).astype(jnp.float32)  10.1 us
  transfers between devices with their start and end apart: 4, of which 4 were waited for; matrix products, arithmetic and copies ran while one was open for 10% of the time, Pallas kernels for 0%

commit v1 on v0

--- a/solution.py
+++ b/solution.py
@@ -6,6 +6,18 @@
 HEADS = 20
 HD = 112
 norm_eps = 1e-06
+
+
+def collect(x, axis, dim):
+    ways, here = (lax.axis_size(axis), lax.axis_index(axis))
+    grown, reach = (x, 1)
+    while reach < ways:
+        theirs = lax.ppermute(grown, axis, [(d, d ^ reach) for d in range(ways)])
+        mine_first = jnp.concatenate([grown, theirs], axis=dim)
+        theirs_first = jnp.concatenate([theirs, grown], axis=dim)
+        grown = jnp.where(here & reach == 0, mine_first, theirs_first)
+        reach = 2 * reach
+    return grown
 
 
 def entering(part, axis, combine, identity):
@@ -98,11 +110,7 @@
     normed = (
         (attended * inv_rms * gain_table).astype(jnp.bfloat16).reshape(frames * tokens, model_width)
     )
-    projected = jnp.dot(
-        normed,
-        lax.all_gather(out_weight, "frm", axis=0, tiled=True),
-        preferred_element_type=jnp.float32,
-    )
+    projected = jnp.dot(normed, collect(out_weight, "frm", 0), preferred_element_type=jnp.float32)
     return projected.astype(jnp.bfloat16).reshape(frames, lat_rows, lat_cols, model_width)
 
 

time: 477 us -> 561 us (1.18)
  blocking collectives: 11.9 us -> 126 us
  waiting for transfers between devices: 327 us -> 289 us
  other arithmetic: 15.5 us -> 23.6 us
    all_gather x1 -> x0, waiting for transfers between devices: 153 us -> none  [local(): lax.all_gather(out_weight, 'frm', axis=0, tiled=True)]
    unnamed x1, blocking collectives: 11.9 us -> 126 us
    all_gather x2, waiting for transfers between devices: 124 us -> 184 us  [entering(): gathered = jax.tree.map(lambda a: lax.all_gather(a, axis), part)]
    ppermute x0 -> x2, waiting for transfers between devices: none -> 56.3 us  [collect(): theirs = lax.ppermute(grown, axis, [(d, d ^ reach) for d in range(ways)])]
    select_n x0 -> x1, other arithmetic: none -> 7.91 us  [collect(): grown = jnp.where(here & reach == 0, mine_first, theirs_first)]
  transfers between devices with their start and end apart: 4 -> 5, of which waited for: 4 -> 3; matrix products, arithmetic and copies ran while one was open for 10% -> 9% of each run, Pallas kernels for 0% -> 0%
where the time goes in v1:
time: 561 us; the launch traced here: 560 us
  waiting for transfers between devices  289 us (52%)
  blocking collectives  126 us (22%)
  local copies, waits for them, and re-layouts  82.3 us (15%)
  other arithmetic  23.6 us (4%)
  matrix products  18.9 us (3%)
  between operations  18.5 us (3%)
    all_gather x2, waiting for transfers between devices, entering(): gathered = jax.tree.map(lambda a: lax.all_gather(a, axis), part)  184 us
    unnamed x1, blocking collectives  126 us
    ppermute x2, waiting for transfers between devices, collect(): theirs = lax.ppermute(grown, axis, [(d, d ^ reach) for d in range(ways)])  56.3 us
    psum x1, waiting for transfers between devices, local(): summed = lax.psum(partial_value, 'row')  48.6 us
    unnamed x18, local copies, waits for them, and re-layouts  24.7 us
    dot_general x1, matrix products, local(): jnp.dot(normed, collect(out_weight, 'frm', 0), preferred_element_type=jnp...  11.4 us
  transfers between devices with their start and end apart: 5, of which 3 were waited for; matrix products, arithmetic and copies ran while one was open for 9% of the time, Pallas kernels for 0%

profile of v1, /device:TPU:0, one launch (start us, length us, event | category | flops | bytes accessed | tf_op | source)
XLA Modules:
  0.0 560.5 jit_solution(14881086034674286296)
XLA Ops:
  6.5 1.8 broadcast_maximum_fusion.1
  8.3 10.3 %copy.16 = bf16[2,2,128,2240]{2,1,3,0:T(2,128)(2,1)} copy(bf16[2,2,128,2240]{2,3,1,0:T(8,128)(2,1)S(1)} %broadcast_maximum_fusion.1) | data formatting | bytes 4587520 | tf_op jit(solution)/shard_map/jit(relu)/max | solution.py:89
  18.7 5.2 reshape.37
  23.9 12.6 %copy.17 = bf16[2,2,128,2240]{2,1,3,0:T(2,128)(2,1)} copy(bf16[2,2,128,2240]{2,3,1,0:T(8,128)(2,1)} %param.11) | data formatting | bytes 4587520 | tf_op args[2]
  36.5 6.2 %reshape.38 = bf16[2,256,20,112]{1,3,2,0:T(8,128)(2,1)} reshape(bf16[2,2,128,2240]{2,1,3,0:T(2,128)(2,1)} %copy.17) | data formatting | bytes 4587520 | tf_op jit(solution)/shard_map/reshape | solution.py:90
  42.7 3.8 fusion.19
  46.5 5.5 reshape.39
  52.1 0.6 dynamic-slice
  52.7 1.2 maximum_dynamic-update-slice_fusion
  55.9 0.6 fusion.18
  56.5 48.6 %all-reduce.3.cloned.1.call-done = f32[2,250880]{1,0:T(2,128)} async-done(((f32[2,250880]{1,0:T(2,128)}), f32[2,250880]{1,0:T(2,128)}) %all-reduce.3.cloned.1.call-update) | async-done | bytes 2007056 | tf_op jit(solution)/shard_map/psum | solution.py:97
  105.1 8.2 %fusion.17 = (f32[1,250880]{1,0:T(1,128)S(1)}, f32[1,1,250880]{2,1,0:T(1,128)}, f32[1,1,250880]{2,1,0:T(1,128)}, f32[1,250880]{1,0:T(1,128)}) fusion(f32[2,250880]{1,0:T(2,128)} %all-reduce.3.cloned.1.call-done, f32[]{:T(128)} %bitcast.7, f32[]{:T(128)} %bitcast.6, f32[]{:T(128)} %bitcast.5, f32[]{:T(128)} %bitcast.12, f32[]{:T(128)} %bitcast.11), kind=kLoop, calls=%fused_computation.37 | loop fusion | flops 1505280 | bytes 6021140 | tf_op jit(solution)/shard_map/slice | solution.py:59
  113.3 0.7 all-gather.6.cloned.1.call-update
  114.0 1.6 collective-permute-start
  115.6 126.1 %all-reduce = f32[4]{0:T(128)S(1)} all-reduce(f32[4]{0:T(128)S(1)} %get-tuple-element.81), channel_id=2, replica_groups=mesh['grp'=2,'frm'=4,'row'=4] {'frm'}, use_global_device_ids=true, to_apply=%add | all-reduce | flops 4 | bytes 32
  241.8 10.1 %copy.20 = bf16[2,2,128,2240]{2,1,3,0:T(2,128)(2,1)S(1)} copy(bf16[2,2,128,2240]{2,3,1,0:T(8,128)(2,1)S(1)} %broadcast_maximum_fusion) | data formatting | bytes 4587520 | tf_op jit(solution)/shard_map/jit(relu)/max | solution.py:104
  251.9 2.7 reshape.40
  254.7 7.9 %maximum_select_fusion.2 = bf16[1120,2240]{1,0:T(8,128)(2,1)} fusion(bf16[560,2240]{1,0:T(8,128)(2,1)} %collective-permute-done, bf16[560,2240]{1,0:T(8,128)(2,1)} %param.14, pred[]{:T(512)S(6)} %eq.7), kind=kLoop, calls=%fused_computation.13 | loop fusion | flops 22579200 | bytes 10035201 | tf_op jit(solution)/shard_map/jit(_where)/select_n | solution.py:18
  262.7 5.5 copy.28
  268.2 183.6 %all-gather.6.cloned.1.call-done = f32[4,1,250880]{2,1,0:T(1,128)} async-done(((f32[1,1,250880]{2,1,0:T(1,128)}), f32[4,1,250880]{2,1,0:T(1,128)}) %all-gather.6.cloned.1.call-update) | async-done | bytes 4014096 | tf_op jit(solution)/shard_map/all_gather | solution.py:25
  451.8 5.5 copy.29
  460.9 3.6 add_add_fusion.1
  464.5 1.8 stack.9
  466.7 3.0 stack.10
  469.7 2.6 copy.19
  472.3 3.7 fusion.7
  476.1 0.7 fusion.9
  476.8 2.4 copy.21
  479.7 56.3 %collective-permute-done.1 = bf16[1120,2240]{1,0:T(8,128)(2,1)} collective-permute-done((bf16[1120,2240]{1,0:T(8,128)(2,1)}, bf16[1120,2240]{1,0:T(8,128)(2,1)}, u32[]{:S(2)}, u32[]{:S(2)}) %collective-permute-start.1) | collective-permute-done | bytes 5017632 | tf_op jit(solution)/shard_map/ppermute | solution.py:15
  536.0 11.4 %fusion.10 = bf16[512,2240]{0,1:T(8,128)(2,1)} fusion(bf16[512,2240]{0,1:T(8,128)(2,1)S(1)} %bitcast.73, bf16[1120,2240]{1,0:T(8,128)(2,1)} %collective-permute-done.1, bf16[1120,2240]{1,0:T(8,128)(2,1)} %maximum_select_fusion.2, pred[]{:T(512)S(6)} %eq.6), kind=kOutput, calls=%fused_computation.19 | convolution fusion | flops 5184327680 | bytes 14622721 | tf_op jit(solution)/shard_map/dot_general | solution.py:113
  547.4 4.8 reshape.42
  552.2 1.7 copy.22
  (31 shorter events, 1.6 us)
Async XLA Ops:
  6.5 98.6 %all-reduce.3.cloned.1.call-start = ((), (), s32[]{:S(2)}) async-start(), calls=%async_computation | async-start | bytes 4014080 | tf_op jit(solution)/shard_map/psum | solution.py:97
  46.5 5.6 %copy-start.3 = (s32[2]{0:T(128)S(1)}, s32[2]{0:T(128)}, u32[]{:S(2)}) copy-start(s32[2]{0:T(128)} %param.13) | copy-start | bytes 28
  46.5 5.7 %copy-start.5 = (u32[32]{0:T(128)S(1)}, u32[32]{0:T(128)}, u32[]{:S(2)}) copy-start(u32[32]{0:T(128)} %constant.56) | copy-start | bytes 388
  46.5 9.4 %copy-start.4 = (s32[2]{0:T(128)S(1)}, s32[2]{0:T(128)}, u32[]{:S(2)}) copy-start(s32[2]{0:T(128)} %param.12) | copy-start | bytes 28
  52.0 210.6 %all-gather.8.cloned.1.call-start = ((), (), s32[]{:S(2)}) async-start(), calls=%async_computation.2 | async-start | bytes 5017600 | tf_op jit(solution)/shard_map/all_gather | solution.py:25
  105.1 136.6 %copy-start.1 = (bf16[2,2,128,2240]{2,3,1,0:T(8,128)(2,1)S(1)}, bf16[2,2,128,2240]{2,3,1,0:T(8,128)(2,1)}, u32[]{:S(2)}) copy-start(bf16[2,2,128,2240]{2,3,1,0:T(8,128)(2,1)} %param.9) | copy-start | bytes 6881284
  113.3 338.5 %all-gather.6.cloned.1.call-start = ((), (), s32[]{:S(2)}) async-start(), calls=%async_computation.1 | async-start | bytes 5017600 | tf_op jit(solution)/shard_map/all_gather | solution.py:25
  114.0 140.7 %collective-permute-start = (bf16[560,2240]{1,0:T(8,128)(2,1)}, bf16[560,2240]{1,0:T(8,128)(2,1)}, u32[]{:S(2)}, u32[]{:S(2)}) collective-permute-start(bf16[560,2240]{1,0:T(8,128)(2,1)} %param.14), channel_id=1, source_target_pairs={{0,4},{4,0},{8,12},{12,8},{1,5},{5,1},{9,13},{13,9},{2,6},{6,2},{1... | collective-permute-start | bytes 7526408 | tf_op jit(solution)/shard_map/ppermute | solution.py:15
  251.9 2.8 copy-start.2
  262.6 273.3 %collective-permute-start.1 = (bf16[1120,2240]{1,0:T(8,128)(2,1)}, bf16[1120,2240]{1,0:T(8,128)(2,1)}, u32[]{:S(2)}, u32[]{:S(2)}) collective-permute-start(bf16[1120,2240]{1,0:T(8,128)(2,1)} %maximum_select_fusion.2), channel_id=1, source_target_pairs={{0,8},{4,12},{8,0},{12,4},{1,9},{5,13},{9,1},{13,5},{2,10},{6,14},... | collective-permute-start | bytes 15052808 | tf_op jit(solution)/shard_map/ppermute | solution.py:15
  466.7 5.6 %copy-start = (bf16[2,256,20,112]{1,3,2,0:T(8,128)(2,1)S(1)}, bf16[2,256,20,112]{1,3,2,0:T(8,128)(2,1)}, u32[]{:S(2)}) copy-start(bf16[2,256,20,112]{1,3,2,0:T(8,128)(2,1)} %reshape.40) | copy-start | bytes 6881284
Sparse Core Ops, SparseCore 0:
  52.1 52.9 all-reduce.2
  113.4 122.2 all-gather.7
  237.3 214.4 all-gather.5
